TPU v7x, 512 devices: a whole 4x8x8 slice. The times are simulated.
512 devices in a mesh: seq: 32 (over y, z_lo, core), row: 4 (over x), col: 4 (over z_hi).
Axes of the slice: x: 4, y: 8, z: 8 (z_hi: 4, z_lo: 2; z = z_hi * 2 + z_lo), core: 2. Of those that a mesh axis runs over, the one named last changes fastest.
Arguments:
- hidden_in: bfloat16 [4, 16384, 1024], P('row', 'seq')
- qkv_weight: bfloat16 [1024, 16, 192], P(None, 'col'), may hold values from -0.1875 to 0.1875
- qkv_global_weight: bfloat16 [1024, 16, 192], P('row', 'col'), may hold values from -0.1875 to 0.1875
- out_weight: bfloat16 [1024, 1024], P('col'), may hold values from -0.75 to 0.75
- ln_gain: float32 [1024], replicated, may hold values from 0.1 to 1.9
- ln_bias: float32 [1024], replicated, may hold values from -3 to 3
- ffn_in: bfloat16 [1024, 4096], P('row', 'col'), may hold values from -0.1875 to 0.1875
- ffn_out: bfloat16 [4096, 1024], P('col', 'row'), may hold values from -0.09375 to 0.09375
- ln2_gain: float32 [1024], replicated, may hold values from 0.1 to 1.9
- ln2_bias: float32 [1024], replicated, may hold values from -3 to 3
- segment_ids: int32 [4, 16384], P('row'), may hold values from 0 to 63, never falling along the last dimension, each value on 1 to 9216 neighbouring positions
- global_pos: int32 [4, 128], P('row'), may hold values from 0 to 16383, as said below
- page_owner: int32 [4, 1024, 1], P('row', 'seq'), may hold values from 0 to 31; in each aligned block of 32 rows (0 to 31, 32 to 63, ..., all dimensions but the last counted through in order) at most 2 rows name the same one
Outputs:
- hidden_out: bfloat16 [4, 16384, 1024], P('row', ('seq', 'col'))
- page_pool: bfloat16 [4, 32, 32, 2, 16, 16, 128], P('row', 'seq', None, None, None, 'col')
Inputs may be any that keep to these rules, and one draw needn't show every extreme that they name: `segment_ids`: in each stream, prompt numbers never fall along positions and every prompt has 1 to 9216 tokens, one exactly 9216. `global_pos`: in each stream, exactly 4 distinct global positions lie in each block of 512 consecutive tokens, listed in increasing order. `page_owner`: among the 32 pages of one shard of a stream, at most 2 have the same owner.
All inputs are finite; a program needn't handle non-finite values.
Results may differ from a plain program's by a relative error of at most 0.014.
The roundings to bfloat16 on the way count: a program that leaves them out, or rounds other values in their place, can miss the bound.
Values may be sent and summed in bfloat16 or wider, within the bound.
A program may use at most 64 MiB of HBM per device.

v0:
```python
import math
import jax
import jax.numpy as jnp
from jax import lax
from jax.sharding import PartitionSpec as P

HALF = 256


def padded(block, sides, width):
    for axis, dim in sides:
        count = lax.axis_size(axis)
        forward = [(i, i + 1) for i in range(count - 1)]
        backward = [(target, source) for source, target in forward]
        low = lax.ppermute(
            lax.slice_in_dim(block, block.shape[dim] - width, None, axis=dim), axis, forward
        )
        high = lax.ppermute(lax.slice_in_dim(block, 0, width, axis=dim), axis, backward)
        block = jnp.concatenate([low, block, high], axis=dim)
    return block


def combined_all(array, axis, combine):
    everything = jax.tree.map(lambda part: lax.all_gather(part, axis), array)
    initial = jax.tree.map(lambda part: part[0], everything)

    def lap(k, so_far):
        return combine(so_far, jax.tree.map(lambda part: part[k], everything))

    return lax.fori_loop(1, lax.axis_size(axis), lap, initial)


def combine_parts(first, second):
    top = jnp.maximum(first[0], second[0])
    left = jnp.exp(first[0] - top)
    right = jnp.exp(second[0] - top)
    return (
        top,
        first[1] * left + second[1] * right,
        first[2] * left[:, :, None] + second[2] * right[:, :, None],
    )


def layer_norm(values, gain, bias):
    center = values - jnp.mean(values, axis=1, keepdims=True)
    spread = jnp.mean(center * center, axis=1, keepdims=True)
    return center * lax.rsqrt(spread + 1e-05) * gain + bias


def per_device(
    hidden_in,
    qkv_weight,
    qkv_global_weight,
    out_weight,
    ln_gain,
    ln_bias,
    ffn_in,
    ffn_out,
    ln2_gain,
    ln2_bias,
    segment_ids,
    global_pos,
    page_owner,
):
    neg = -1e30
    tokens = hidden_in[0]
    shard_len, width = tokens.shape
    heads_here = qkv_weight.shape[1]
    triple = qkv_weight.shape[2]
    head_dim = triple // 3
    n_seq = lax.axis_size("seq")
    n_col = lax.axis_size("col")
    seq_index = lax.axis_index("seq")
    col_index = lax.axis_index("col")
    base = seq_index * shard_len
    scale = 1.0 / math.sqrt(head_dim)
    qkv = jnp.dot(
        tokens, qkv_weight.reshape(width, heads_here * triple), preferred_element_type=jnp.float32
    ).astype(jnp.bfloat16)
    qkv_heads = qkv.reshape(shard_len, heads_here, triple)
    queries = qkv_heads[:, :, :head_dim]
    kv_local = qkv_heads[:, :, head_dim:]
    piece = lax.all_gather(qkv_global_weight, "row", axis=0, tiled=True)
    cols = tokens
    global_proj = jnp.dot(
        cols, piece.reshape(piece.shape[0], heads_here * triple), preferred_element_type=jnp.float32
    )
    global_heads = global_proj.astype(jnp.bfloat16).reshape(shard_len, heads_here, triple)
    global_query_local = global_heads[:, :, :head_dim]
    global_kv_local = global_heads[:, :, head_dim:]
    owners = page_owner[0, :, 0]
    n_pages = owners.shape[0]
    page_len = shard_len // n_pages
    capacity = max(2, n_pages // n_seq)
    page_order = jnp.arange(n_pages, dtype=jnp.int32)
    slot = jnp.sum(
        ((owners[:, None] == owners[None, :]) & (page_order[None, :] < page_order[:, None])).astype(
            jnp.int32
        ),
        axis=1,
    )
    target = owners * capacity + slot
    placing = (target[None, :] == jnp.arange(n_seq * capacity, dtype=jnp.int32)[:, None]).astype(
        jnp.bfloat16
    )
    outgoing = jnp.dot(
        placing,
        kv_local.reshape(n_pages, page_len * heads_here * 2 * head_dim),
        preferred_element_type=jnp.float32,
    ).astype(jnp.bfloat16)
    outgoing = outgoing.reshape(n_seq, capacity, page_len, heads_here, 2 * head_dim)
    arrived = lax.all_to_all(outgoing, "seq", split_axis=0, concat_axis=0, tiled=True)
    page_pool = arrived[None, None]
    kv_ext = padded(kv_local, (("seq", 0),), HALF)
    all_pos = global_pos[0]
    n_glob = all_pos.shape[0]
    per_shard = n_glob // n_seq
    own_pos = lax.dynamic_slice_in_dim(all_pos, seq_index * per_shard, per_shard, 0)
    local_order = jnp.arange(shard_len, dtype=jnp.int32)
    own_match = (own_pos - base)[:, None] == local_order[None, :]
    picker = own_match.astype(jnp.bfloat16)
    own_kv = jnp.dot(
        picker,
        kv_local.reshape(shard_len, heads_here * 2 * head_dim),
        preferred_element_type=jnp.float32,
    ).astype(jnp.bfloat16)
    own_query = jnp.dot(
        picker,
        global_query_local.reshape(shard_len, heads_here * head_dim),
        preferred_element_type=jnp.float32,
    ).astype(jnp.bfloat16)
    gathered = (
        lax.all_gather(own_kv, "seq", axis=0, tiled=True),
        lax.all_gather(own_query, "seq", axis=0, tiled=True),
    )
    glob_kv = gathered[0].reshape(n_glob, heads_here, 2 * head_dim)
    glob_q = gathered[1].reshape(n_glob, heads_here, head_dim)
    glob_k = glob_kv[:, :, :head_dim]
    glob_v = glob_kv[:, :, head_dim:]
    seg_all = segment_ids[0]
    glob_seg = jnp.take(seg_all, all_pos)
    seg_pad = jnp.pad(seg_all, (HALF, HALF), constant_values=-1)
    query_seg = lax.dynamic_slice_in_dim(seg_all, base, shard_len, 0)
    key_seg = lax.dynamic_slice_in_dim(seg_pad, base, shard_len + 2 * HALF, 0)
    key_pos = base - HALF + jnp.arange(shard_len + 2 * HALF, dtype=jnp.int32)
    key_flag = jnp.any(key_pos[:, None] == all_pos[None, :], axis=1)
    query_pos = base + local_order
    glob_mask = query_seg[:, None] == glob_seg[None, :]
    block = min(shard_len, 512)
    k_blk = kv_ext[0 : block + 2 * HALF, :, :head_dim]
    v_blk = kv_ext[0 : block + 2 * HALF, :, head_dim:]
    s_win = jnp.einsum("qhd,khd->hqk", queries, k_blk, preferred_element_type=jnp.float32) * scale
    s_glob = jnp.einsum("qhd,ghd->hqg", queries, glob_k, preferred_element_type=jnp.float32) * scale
    m_win = (
        (jnp.abs(query_pos[:, None] - key_pos[None, :]) <= HALF)
        & (query_seg[0:block, None] == key_seg[None, 0 : block + 2 * HALF])
        & jnp.logical_not(key_flag[None, 0 : block + 2 * HALF])
    )
    top = jnp.maximum(
        jnp.max(jnp.where(m_win, s_win, neg), axis=2),
        jnp.max(jnp.where(glob_mask, s_glob, neg), axis=2),
    )
    e_win = jnp.where(m_win, jnp.exp(s_win - top[:, :, None]), 0.0)
    e_glob = jnp.where(glob_mask, jnp.exp(s_glob - top[:, :, None]), 0.0)
    total = jnp.sum(e_win, axis=2) + jnp.sum(e_glob, axis=2)
    numer = jnp.einsum(
        "hqk,khd->qhd", e_win.astype(jnp.bfloat16), v_blk, preferred_element_type=jnp.float32
    )
    numer = numer + jnp.einsum(
        "hqg,ghd->qhd", e_glob.astype(jnp.bfloat16), glob_v, preferred_element_type=jnp.float32
    )
    pieces = (numer / jnp.transpose(total)[:, :, None]).astype(jnp.bfloat16)
    s_part = (
        jnp.einsum(
            "ghd,khd->hgk",
            glob_q,
            global_kv_local[:, :, :head_dim],
            preferred_element_type=jnp.float32,
        )
        * scale
    )
    part_mask = glob_seg[:, None] == query_seg[None, :]
    part_top = jnp.max(jnp.where(part_mask, s_part, neg), axis=2)
    e_part = jnp.where(part_mask, jnp.exp(s_part - part_top[:, :, None]), 0.0)
    part_total = jnp.sum(e_part, axis=2)
    part_acc = jnp.einsum(
        "hgk,khd->hgd",
        e_part,
        global_kv_local[:, :, head_dim:].astype(jnp.float32),
        precision=lax.Precision.HIGHEST,
    )
    merged = combined_all((part_top, part_total, part_acc), "seq", combine_parts)
    glob_out = (merged[2] / merged[1][:, :, None]).astype(jnp.bfloat16)
    own_out = lax.dynamic_slice_in_dim(glob_out, seq_index * per_shard, per_shard, 1)
    placed = jnp.einsum("gt,hgd->thd", picker, own_out, preferred_element_type=jnp.float32).astype(
        jnp.bfloat16
    )
    is_own = jnp.any(own_match, axis=0)
    attention = jnp.where(is_own[:, None, None], placed, pieces).reshape(
        shard_len, heads_here * head_dim
    )
    out_rows = shard_len // n_col
    proj = lax.psum_scatter(
        jnp.dot(attention, out_weight, preferred_element_type=jnp.float32).astype(jnp.bfloat16),
        "col",
        scatter_dimension=0,
        tiled=True,
    ).astype(jnp.float32)
    residual = lax.dynamic_slice_in_dim(tokens, col_index * out_rows, out_rows, 0).astype(
        jnp.float32
    )
    middle = layer_norm(residual + proj, ln_gain, ln_bias).astype(jnp.bfloat16)
    middle_all = lax.all_gather(middle, "col", axis=0, tiled=True)
    cols = middle_all
    ffn_pre = jnp.dot(
        cols, lax.all_gather(ffn_in, "row", axis=0, tiled=True), preferred_element_type=jnp.float32
    )
    ffn_hidden = jax.nn.gelu(ffn_pre, approximate=False).astype(jnp.bfloat16)
    down_full = lax.all_gather(ffn_out, "row", axis=1, tiled=True)
    ffn_part = lax.psum_scatter(
        jnp.dot(ffn_hidden, down_full, preferred_element_type=jnp.float32).astype(jnp.bfloat16),
        "col",
        scatter_dimension=0,
        tiled=True,
    ).astype(jnp.float32)
    second = middle.astype(jnp.float32) + ffn_part
    normed = layer_norm(second, ln2_gain, ln2_bias)
    return (normed.astype(jnp.bfloat16)[None], page_pool)


def solution(mesh):
    in_specs = (
        P("row", "seq", None),
        P(None, "col", None),
        P("row", "col", None),
        P("col", None),
        P(),
        P(),
        P("row", "col"),
        P("col", "row"),
        P(),
        P(),
        P("row", None),
        P("row", None),
        P("row", "seq", None),
    )
    out_specs = (P("row", ("seq", "col"), None), P("row", "seq", None, None, None, "col", None))
    return jax.shard_map(
        per_device, mesh=mesh, in_specs=in_specs, out_specs=out_specs, check_vma=False
    )
```

profile of v0, /device:TPU:8, one launch (start us, length us, event | category | flops | bytes accessed | tf_op | source)
XLA Modules:
  0.0 483.1 jit_solution(8521363212529290202)
XLA Ops:
  8.6 1.8 gather_fusion
  12.6 37.6 %all-gather.13.cloned.1.call-done = bf16[1024,4,192]{0,2,1:T(8,128)(2,1)} async-done(((bf16[256,4,192]{0,2,1:T(8,128)(2,1)}), bf16[1024,4,192]{0,2,1:T(8,128)(2,1)}) %all-gather.13.cloned.1.call-update) | async-done | bytes 1572880 | tf_op jit(solution)/shard_map/all_gather | solution.py:83
  50.2 3.6 convolution_convert_fusion.4
  53.8 1.4 copy.53
  55.4 32.3 %all-gather.3 = bf16[32,4,256]{2,1,0:T(4,128)(2,1)S(1)} all-gather(bf16[1,4,256]{2,1,0:T(4,128)(2,1)S(1)} %fusion.28), channel_id=1, replica_groups=mesh['seq'=32,'row'=4,'col'=4] {'seq'}, dimensions={0}, use_global_device_ids=true | all-gather | bytes 67584 | tf_op jit(solution)/shard_map/all_gather | solution.py:134
  88.2 1.0 copy-done.3
  89.2 1.6 fusion.68
  90.9 3.1 convolution_convert_fusion.3
  94.1 1.4 copy.57
  96.2 2.2 collective-permute-start
  98.5 4.2 collective-permute-start.1
  103.5 32.5 %all-gather.6 = bf16[32,4,512]{2,1,0:T(4,128)(2,1)S(1)} all-gather(bf16[1,4,512]{2,1,0:T(4,128)(2,1)S(1)} %fusion.27), channel_id=1, replica_groups=mesh['seq'=32,'row'=4,'col'=4] {'seq'}, dimensions={0}, use_global_device_ids=true | all-gather | bytes 135168 | tf_op jit(solution)/shard_map/all_gather | solution.py:133
  137.5 1.2 pad_maximum_fusion
  138.7 1.7 select_reduce_fusion
  140.6 2.7 fusion.3
  143.7 2.1 fusion.65
  146.2 31.2 %all-gather.5 = f32[32,4,128]{2,1,0:T(4,128)S(1)} all-gather(f32[1,4,128]{2,1,0:T(4,128)S(1)} %bitcast.109), channel_id=3, replica_groups=mesh['seq'=32,'row'=4,'col'=4] {'seq'}, dimensions={0}, use_global_device_ids=true | all-gather | bytes 67584 | tf_op jit(solution)/shard_map/all_gather | solution.py:24
  177.3 31.9 %all-gather.4 = f32[32,4,128]{2,1,0:T(4,128)S(1)} all-gather(f32[1,4,128]{2,1,0:T(4,128)S(1)} %bitcast.108), channel_id=2, replica_groups=mesh['seq'=32,'row'=4,'col'=4] {'seq'}, dimensions={0}, use_global_device_ids=true | all-gather | bytes 67584 | tf_op jit(solution)/shard_map/all_gather | solution.py:24
  210.3 42.2 %while.19 = (s32[]{:T(128)}, f32[4,128]{1,0:T(4,128)S(1)}, f32[4,128]{1,0:T(4,128)S(1)}, f32[4,128,64]{2,1,0:T(8,128)S(1)}, f32[32,4,128]{2,1,0:T(4,128)S(1)}, /...) while((s32[]{:T(128)}, f32[4,128]{1,0:T(4,128)S(1)}, ...), condition=%wide.region_4.5_spmd, body=%wide.region_3.4_spmd.sunk | while | flops 101381 | bytes 938135 | solution.py:30
  210.3 0.9 constant_dynamic-slice_fusion.5
  211.7 0.9 constant_dynamic-slice_fusion.5
  213.1 0.9 constant_dynamic-slice_fusion.5
  214.4 0.9 constant_dynamic-slice_fusion.5
  215.8 0.9 constant_dynamic-slice_fusion.5
  217.2 0.9 constant_dynamic-slice_fusion.5
  218.5 0.9 constant_dynamic-slice_fusion.5
  219.9 0.9 constant_dynamic-slice_fusion.5
  221.2 0.9 constant_dynamic-slice_fusion.5
  222.6 0.9 constant_dynamic-slice_fusion.5
  224.0 0.9 constant_dynamic-slice_fusion.5
  225.3 0.9 constant_dynamic-slice_fusion.5
  226.7 0.9 constant_dynamic-slice_fusion.5
  228.1 0.9 constant_dynamic-slice_fusion.5
  229.4 0.9 constant_dynamic-slice_fusion.5
  230.8 0.9 constant_dynamic-slice_fusion.5
  232.1 0.9 constant_dynamic-slice_fusion.5
  233.5 0.9 constant_dynamic-slice_fusion.5
  234.9 0.9 constant_dynamic-slice_fusion.5
  236.2 0.9 constant_dynamic-slice_fusion.5
  237.6 0.9 constant_dynamic-slice_fusion.5
  239.0 0.9 constant_dynamic-slice_fusion.5
  240.3 0.9 constant_dynamic-slice_fusion.5
  241.7 0.9 constant_dynamic-slice_fusion.5
  243.0 0.9 constant_dynamic-slice_fusion.5
  244.4 0.9 constant_dynamic-slice_fusion.5
  245.8 0.9 constant_dynamic-slice_fusion.5
  247.1 0.9 constant_dynamic-slice_fusion.5
  248.5 0.9 constant_dynamic-slice_fusion.5
  253.0 2.6 convolution_convert_fusion.2
  256.8 38.2 %reduce-scatter.3.cloned.1.call-done = bf16[128,1024]{1,0:T(8,128)(2,1)} async-done(((bf16[512,1024]{1,0:T(8,128)(2,1)}), bf16[128,1024]{1,0:T(8,128)(2,1)}) %reduce-scatter.3.cloned.1.call-update) | async-done | bytes 262160 | tf_op jit(solution)/shard_map/reduce_scatter | solution.py:203
  295.0 1.1 fusion.86
  296.1 1.2 multiply_reduce_fusion.1
  297.3 1.8 add_convert_fusion.1
  300.3 31.9 %all-gather.17.cloned.1.call-done = bf16[1024,1024]{1,0:T(8,128)(2,1)} async-done(((bf16[256,1024]{1,0:T(8,128)(2,1)}), bf16[1024,1024]{1,0:T(8,128)(2,1)}) %all-gather.17.cloned.1.call-update) | async-done | bytes 2097168 | tf_op jit(solution)/shard_map/all_gather | solution.py:216
  332.2 42.1 %all-gather.19.cloned.1.call-done = bf16[1024,1024]{1,0:T(8,128)(2,1)} async-done(((bf16[1024,256]{1,0:T(8,128)(2,1)}), bf16[1024,1024]{1,0:T(8,128)(2,1)}) %all-gather.19.cloned.1.call-update) | async-done | bytes 2097168 | tf_op jit(solution)/shard_map/all_gather | solution.py:219
  374.3 40.8 %all-gather.15.cloned.1.call-done = bf16[512,1024]{1,0:T(8,128)(2,1)} async-done(((bf16[128,1024]{1,0:T(8,128)(2,1)}), bf16[512,1024]{1,0:T(8,128)(2,1)}) %all-gather.15.cloned.1.call-update) | async-done | bytes 1048592 | tf_op jit(solution)/shard_map/all_gather | solution.py:213
  415.1 9.8 %convolution_convert_fusion.1 = bf16[512,1024]{1,0:T(8,128)(2,1)} fusion(bf16[1024,1024]{1,0:T(8,128)(2,1)} %all-gather.19.cloned.1.call-done, bf16[512,1024]{1,0:T(8,128)(2,1)} %all-gather.15.cloned.1.call-done, bf16[1024,1024]{1,0:T(8,128)(2,1)} %all-gather.17.cloned.1.call-done), kind=kOutput, calls=%fused_computation.39 | convolution fusion | flops 2182086656 | bytes 6291456 | tf_op jit(solution)/shard_map/dot_general | solution.py:221
  425.3 1.6 reshape.176
  426.9 37.3 %all_to_all.5 = bf16[32,2,16,4,128]{4,3,2,1,0:T(4,128)(2,1)S(1)} all-to-all(bf16[32,2,16,4,128]{4,3,2,1,0:T(4,128)(2,1)} %reshape.176), channel_id=1, replica_groups=mesh['seq'=32,'row'=4,'col'=4] {'seq'}, dimensions={0} | all-to-all | bytes 2097152 | tf_op jit(solution)/shard_map/all_to_all | solution.py:112
  464.1 7.0 %reduce-scatter.5.cloned.1.call-done = bf16[128,1024]{1,0:T(8,128)(2,1)} async-done(((bf16[512,1024]{1,0:T(8,128)(2,1)}), bf16[128,1024]{1,0:T(8,128)(2,1)}) %reduce-scatter.5.cloned.1.call-update) | async-done | bytes 262160 | tf_op jit(solution)/shard_map/reduce_scatter | solution.py:220
  471.2 1.1 fusion.84
  472.3 1.2 multiply_reduce_fusion
  473.5 1.8 fusion.87
  475.3 1.0 copy.91
  (179 shorter events, 27.1 us)
Async XLA Ops:
  7.2 83.7 %copy-start = (bf16[1024,4,192]{0,2,1:T(8,128)(2,1)S(1)}, bf16[1024,4,192]{0,2,1:T(8,128)(2,1)}, u32[]{:S(2)}) copy-start(bf16[1024,4,192]{0,2,1:T(8,128)(2,1)} %param.16) | copy-start | bytes 4718596
  7.2 43.0 %all-gather.13.cloned.1.call-start = ((), (), s32[]{:S(2)}) async-start(), calls=%async_computation.3 | async-start | bytes 1966080 | tf_op jit(solution)/shard_map/all_gather | solution.py:83
  7.9 201.3 %all-gather.21.cloned.1.call-start = ((), (), s32[]{:S(2)}) async-start(), calls=%async_computation.9 | async-start | bytes 4325376 | tf_op jit(solution)/shard_map/all_gather | solution.py:24
  88.2 1.0 copy-start.3
  90.9 204.2 %reduce-scatter.3.cloned.1.call-start = ((), (), s32[]{:S(2)}) async-start(), calls=%async_computation.4 | async-start | bytes 1310720 | tf_op jit(solution)/shard_map/reduce_scatter | solution.py:203
  94.0 8.7 %copy-start.2 = (s32[1,16384]{1,0:T(1,128)S(1)}, s32[1,16384]{1,0:T(1,128)}, u32[]{:S(2)}) copy-start(s32[1,16384]{1,0:T(1,128)} %param.25) | copy-start | bytes 196612
  94.0 8.8 %copy-start.10 = (s32[1,128]{1,0:T(1,128)S(1)}, s32[1,128]{1,0:T(1,128)}, u32[]{:S(2)}) copy-start(s32[1,128]{1,0:T(1,128)} %param.26) | copy-start | bytes 1540
  96.2 41.3 %collective-permute-start = (bf16[256,4,128]{0,2,1:T(8,128)(2,1)}, bf16[256,4,128]{0,2,1:T(8,128)(2,1)}, u32[]{:S(2)}, u32[]{:S(2)}) collective-permute-start(bf16[256,4,128]{0,2,1:T(8,128)(2,1)} %get-tuple-element.234), channel_id=1, source_target_pairs={{0,16},{16,32},{32,48},{48,64},{64,80},{80,96},{96,112},{112,128},... | collective-permute-start | bytes 786440 | tf_op jit(solution)/shard_map/ppermute | solution.py:15
  98.5 39.0 %collective-permute-start.1 = (bf16[256,4,128]{0,2,1:T(8,128)(2,1)S(1)}, bf16[256,4,128]{0,2,1:T(8,128)(2,1)}, u32[]{:S(2)}, u32[]{:S(2)}) collective-permute-start(bf16[256,4,128]{0,2,1:T(8,128)(2,1)S(1)} %get-tuple-element.235), channel_id=1, source_target_pairs={{16,0},{32,16},{48,32},{64,48},{80,64},{96,80},{112,96},{128,112},... | collective-permute-start | bytes 786440 | tf_op jit(solution)/shard_map/ppermute | solution.py:18
  143.7 2.1 copy-start.4
  253.0 42.0 %copy-start.5 = (bf16[1,512,1024]{2,1,0:T(8,128)(2,1)S(1)}, bf16[1,512,1024]{2,1,0:T(8,128)(2,1)}, u32[]{:S(2)}) copy-start(bf16[1,512,1024]{2,1,0:T(8,128)(2,1)} %param.15) | copy-start | bytes 3145732
  253.0 44.3 %copy-start.6 = (f32[1024]{0:T(1024)S(1)}, f32[1024]{0:T(1024)}, u32[]{:S(2)}) copy-start(f32[1024]{0:T(1024)} %param.20) | copy-start | bytes 12292
  253.0 44.3 %copy-start.7 = (f32[1024]{0:T(1024)S(1)}, f32[1024]{0:T(1024)}, u32[]{:S(2)}) copy-start(f32[1024]{0:T(1024)} %param.19) | copy-start | bytes 12292
  255.6 76.7 %all-gather.17.cloned.1.call-start = ((), (), s32[]{:S(2)}) async-start(), calls=%async_computation.6 | async-start | bytes 2621440 | tf_op jit(solution)/shard_map/all_gather | solution.py:216
  256.2 118.1 %all-gather.19.cloned.1.call-start = ((), (), s32[]{:S(2)}) async-start(), calls=%async_computation.7 | async-start | bytes 2621440 | tf_op jit(solution)/shard_map/all_gather | solution.py:219
  256.8 158.4 %all-gather.15.cloned.1.call-start = ((), (), s32[]{:S(2)}) async-start(), calls=%async_computation.5 | async-start | bytes 1310720 | tf_op jit(solution)/shard_map/all_gather | solution.py:213
  256.8 43.3 %copy-start.11 = (s32[1,32,1]{1,2,0:T(1,128)S(1)}, s32[1,32,1]{1,2,0:T(1,128)}, u32[]{:S(2)}) copy-start(s32[1,32,1]{1,2,0:T(1,128)} %param.27) | copy-start | bytes 388
  299.1 172.0 %reduce-scatter.5.cloned.1.call-start = ((), (), s32[]{:S(2)}) async-start(), calls=%async_computation.8 | async-start | bytes 1310720 | tf_op jit(solution)/shard_map/reduce_scatter | solution.py:220
  425.3 45.9 %copy-start.1 = (bf16[128,1024]{1,0:T(8,128)(2,1)S(1)}, bf16[128,1024]{1,0:T(8,128)(2,1)}, u32[]{:S(2)}) copy-start(bf16[128,1024]{1,0:T(8,128)(2,1)} %add_convert_fusion.1) | copy-start | bytes 786436
  426.9 46.6 %copy-start.8 = (f32[1024]{0:T(1024)S(1)}, f32[1024]{0:T(1024)}, u32[]{:S(2)}) copy-start(f32[1024]{0:T(1024)} %param.24) | copy-start | bytes 12292
  426.9 46.6 %copy-start.9 = (f32[1024]{0:T(1024)S(1)}, f32[1024]{0:T(1024)}, u32[]{:S(2)}) copy-start(f32[1024]{0:T(1024)} %param.23) | copy-start | bytes 12292
Sparse Core Ops, SparseCore 0:
  10.1 40.0 all-gather.12
  91.0 68.8 all-gather.20
  255.7 39.2 reduce-scatter.2
  297.2 35.0 all-gather.16
  334.4 39.8 all-gather.18
  377.1 38.0 all-gather.14
  425.0 46.1 reduce-scatter.4
where the time goes:
time: 484 us; the launch traced here: 483 us
  waiting for transfers between devices  199 us (41%)
  blocking collectives  165 us (34%)
  local copies, waits for them, and re-layouts  44.3 us (9%)
  matrix products  26.6 us (5%)
  other arithmetic  25.1 us (5%)
  between operations  14.5 us (3%)
  starting transfers between devices  6.95 us (1%)
    all_gather x2, blocking collectives, combined_all(): everything = jax.tree.map(lambda part: lax.all_gather(part, axis), array)  63.1 us
    all_gather x1, waiting for transfers between devices, per_device(): down_full = lax.all_gather(ffn_out, 'row', axis=1, tiled=True)  42.1 us
    all_gather x1, waiting for transfers between devices, per_device(): middle_all = lax.all_gather(middle, 'col', axis=0, tiled=True)  40.8 us
    reduce_scatter x1, waiting for transfers between devices, per_device(): lax.psum_scatter(jnp.dot(attention, out_weight, preferred_element_type=jn...  38.2 us
    all_gather x1, waiting for transfers between devices, per_device(): piece = lax.all_gather(qkv_global_weight, 'row', axis=0, tiled=True)  37.6 us
    all_to_all x1, blocking collectives, per_device(): lax.all_to_all(outgoing, 'seq', split_axis=0, concat_axis=0, tiled=True)  37.3 us
    all_gather x1, blocking collectives, per_device(): lax.all_gather(own_kv, 'seq', axis=0, tiled=True)  32.5 us
    dynamic_slice x62, local copies, waits for them, and re-layouts, lap(): return combine(so_far, jax.tree.map(lambda part: part[k], everything))  32.5 us
  transfers between devices with their start and end apart: 9, of which 6 were waited for; matrix products, arithmetic and copies ran while one was open for 6% of the time, Pallas kernels for 0%

commit v1 on v0

--- a/solution.py
+++ b/solution.py
@@ -5,6 +5,22 @@
 from jax.sharding import PartitionSpec as P
 
 HALF = 256
+
+
+def gather_around(x, axis, dim):
+    ways, here, step = (lax.axis_size(axis), lax.axis_index(axis), x.shape[dim])
+    shape = [n * ways if d == dim else n for d, n in enumerate(x.shape)]
+    full = lax.dynamic_update_slice_in_dim(jnp.zeros(shape, x.dtype), x, here * step, axis=dim)
+    going_up = going_down = x
+    for far in range(1, ways // 2 + 1):
+        going_up = lax.ppermute(going_up, axis, [(d, (d + 1) % ways) for d in range(ways)])
+        full = lax.dynamic_update_slice_in_dim(full, going_up, (here - far) % ways * step, axis=dim)
+        if 2 * far < ways:
+            going_down = lax.ppermute(going_down, axis, [(d, (d - 1) % ways) for d in range(ways)])
+            full = lax.dynamic_update_slice_in_dim(
+                full, going_down, (here + far) % ways * step, axis=dim
+            )
+    return full
 
 
 def padded(block, sides, width):
@@ -212,9 +228,7 @@
     middle = layer_norm(residual + proj, ln_gain, ln_bias).astype(jnp.bfloat16)
     middle_all = lax.all_gather(middle, "col", axis=0, tiled=True)
     cols = middle_all
-    ffn_pre = jnp.dot(
-        cols, lax.all_gather(ffn_in, "row", axis=0, tiled=True), preferred_element_type=jnp.float32
-    )
+    ffn_pre = jnp.dot(cols, gather_around(ffn_in, "row", 0), preferred_element_type=jnp.float32)
     ffn_hidden = jax.nn.gelu(ffn_pre, approximate=False).astype(jnp.bfloat16)
     down_full = lax.all_gather(ffn_out, "row", axis=1, tiled=True)
     ffn_part = lax.psum_scatter(

time: 484 us -> 456 us (0.942)
  the two profiles are of different devices: /device:TPU:8 before, /device:TPU:4 now
where the time goes in v1:
time: 456 us; the launch traced here: 455 us
  blocking collectives  170 us (37%)
  waiting for transfers between devices  151 us (33%)
  local copies, waits for them, and re-layouts  51.3 us (11%)
  matrix products  28.4 us (6%)
  other arithmetic  25.1 us (6%)
  between operations  14.5 us (3%)
  starting transfers between devices  12.9 us (3%)
    all_gather x2, blocking collectives, combined_all(): everything = jax.tree.map(lambda part: lax.all_gather(part, axis), array)  65.1 us
    all_gather x1, waiting for transfers between devices, per_device(): middle_all = lax.all_gather(middle, 'col', axis=0, tiled=True)  42 us
    all_to_all x1, blocking collectives, per_device(): lax.all_to_all(outgoing, 'seq', split_axis=0, concat_axis=0, tiled=True)  38 us
    all_gather x1, waiting for transfers between devices, per_device(): piece = lax.all_gather(qkv_global_weight, 'row', axis=0, tiled=True)  37.4 us
    reduce_scatter x1, waiting for transfers between devices, per_device(): lax.psum_scatter(jnp.dot(attention, out_weight, preferred_element_type=jn...  36.9 us
    all_gather x1, blocking collectives, per_device(): lax.all_gather(own_query, 'seq', axis=0, tiled=True)  34.4 us
    all_gather x1, blocking collectives, per_device(): lax.all_gather(own_kv, 'seq', axis=0, tiled=True)  32.9 us
    dynamic_slice x62, local copies, waits for them, and re-layouts, lap(): return combine(so_far, jax.tree.map(lambda part: part[k], everything))  32.5 us
  transfers between devices with their start and end apart: 11, of which 7 were waited for; matrix products, arithmetic and copies ran while one was open for 8% of the time, Pallas kernels for 0%

profile of v1, /device:TPU:4, one launch (start us, length us, event | category | flops | bytes accessed | tf_op | source)
XLA Modules:
  0.0 454.9 jit_solution(6258302822671567501)
XLA Ops:
  8.6 1.8 gather_fusion
  12.6 37.4 %all-gather.12.cloned.1.call-done = bf16[1024,4,192]{0,2,1:T(8,128)(2,1)} async-done(((bf16[256,4,192]{0,2,1:T(8,128)(2,1)}), bf16[1024,4,192]{0,2,1:T(8,128)(2,1)}) %all-gather.12.cloned.1.call-update) | async-done | bytes 1572880 | tf_op jit(solution)/shard_map/all_gather | solution.py:99
  50.0 3.6 convolution_convert_fusion.4
  53.6 1.4 copy.53
  55.2 34.4 %all-gather.3 = bf16[32,4,256]{2,1,0:T(4,128)(2,1)S(1)} all-gather(bf16[1,4,256]{2,1,0:T(4,128)(2,1)S(1)} %fusion.28), channel_id=1, replica_groups=mesh['seq'=32,'row'=4,'col'=4] {'seq'}, dimensions={0}, use_global_device_ids=true | all-gather | bytes 67584 | tf_op jit(solution)/shard_map/all_gather | solution.py:150
  90.2 1.0 copy-done.3
  91.1 1.6 fusion.68
  92.8 3.1 convolution_convert_fusion.3
  96.0 1.4 copy.57
  98.1 2.9 collective-permute-start
  101.1 1.3 collective-permute-start.1
  103.1 32.9 %all-gather.6 = bf16[32,4,512]{2,1,0:T(4,128)(2,1)S(1)} all-gather(bf16[1,4,512]{2,1,0:T(4,128)(2,1)S(1)} %fusion.27), channel_id=1, replica_groups=mesh['seq'=32,'row'=4,'col'=4] {'seq'}, dimensions={0}, use_global_device_ids=true | all-gather | bytes 135168 | tf_op jit(solution)/shard_map/all_gather | solution.py:149
  137.6 1.2 pad_maximum_fusion
  138.8 1.7 select_reduce_fusion
  140.7 2.7 fusion.3
  143.8 2.9 fusion.65
  147.1 31.2 %all-gather.5 = f32[32,4,128]{2,1,0:T(4,128)S(1)} all-gather(f32[1,4,128]{2,1,0:T(4,128)S(1)} %bitcast.109), channel_id=3, replica_groups=mesh['seq'=32,'row'=4,'col'=4] {'seq'}, dimensions={0}, use_global_device_ids=true | all-gather | bytes 67584 | tf_op jit(solution)/shard_map/all_gather | solution.py:40
  178.2 33.9 %all-gather.4 = f32[32,4,128]{2,1,0:T(4,128)S(1)} all-gather(f32[1,4,128]{2,1,0:T(4,128)S(1)} %bitcast.108), channel_id=2, replica_groups=mesh['seq'=32,'row'=4,'col'=4] {'seq'}, dimensions={0}, use_global_device_ids=true | all-gather | bytes 67584 | tf_op jit(solution)/shard_map/all_gather | solution.py:40
  213.2 42.2 %while.19 = (s32[]{:T(128)}, f32[4,128]{1,0:T(4,128)S(1)}, f32[4,128]{1,0:T(4,128)S(1)}, f32[4,128,64]{2,1,0:T(8,128)S(1)}, f32[32,4,128]{2,1,0:T(4,128)S(1)}, /...) while((s32[]{:T(128)}, f32[4,128]{1,0:T(4,128)S(1)}, ...), condition=%wide.region_4.5_spmd, body=%wide.region_3.4_spmd.sunk | while | flops 101381 | bytes 938135 | solution.py:46
  213.3 0.9 constant_dynamic-slice_fusion.5
  214.6 0.9 constant_dynamic-slice_fusion.5
  216.0 0.9 constant_dynamic-slice_fusion.5
  217.4 0.9 constant_dynamic-slice_fusion.5
  218.7 0.9 constant_dynamic-slice_fusion.5
  220.1 0.9 constant_dynamic-slice_fusion.5
  221.5 0.9 constant_dynamic-slice_fusion.5
  222.8 0.9 constant_dynamic-slice_fusion.5
  224.2 0.9 constant_dynamic-slice_fusion.5
  225.5 0.9 constant_dynamic-slice_fusion.5
  226.9 0.9 constant_dynamic-slice_fusion.5
  228.3 0.9 constant_dynamic-slice_fusion.5
  229.6 0.9 constant_dynamic-slice_fusion.5
  231.0 0.9 constant_dynamic-slice_fusion.5
  232.4 0.9 constant_dynamic-slice_fusion.5
  233.7 0.9 constant_dynamic-slice_fusion.5
  235.1 0.9 constant_dynamic-slice_fusion.5
  236.4 0.9 constant_dynamic-slice_fusion.5
  237.8 0.9 constant_dynamic-slice_fusion.5
  239.2 0.9 constant_dynamic-slice_fusion.5
  240.5 0.9 constant_dynamic-slice_fusion.5
  255.6 1.4 fusion.26
  257.0 2.5 convolution_convert_fusion.2
  260.1 36.9 %reduce-scatter.3.cloned.1.call-done = bf16[128,1024]{1,0:T(8,128)(2,1)} async-done(((bf16[512,1024]{1,0:T(8,128)(2,1)}), bf16[128,1024]{1,0:T(8,128)(2,1)}) %reduce-scatter.3.cloned.1.call-update) | async-done | bytes 262160 | tf_op jit(solution)/shard_map/reduce_scatter | solution.py:219
  297.0 1.1 fusion.86
  298.1 1.2 multiply_reduce_fusion.1
  299.3 1.8 add_convert_fusion.1
  301.2 3.2 collective-permute-start.2
  304.4 2.8 collective-permute-start.3
  307.2 1.6 broadcast_in_dim.109
  309.6 9.9 %collective-permute-done.2 = bf16[256,1024]{1,0:T(8,128)(2,1)} collective-permute-done((bf16[256,1024]{1,0:T(8,128)(2,1)}, bf16[256,1024]{1,0:T(8,128)(2,1)}, u32[]{:S(2)}, u32[]{:S(2)}) %collective-permute-start.2) | collective-permute-done | bytes 524320 | tf_op jit(solution)/shard_map/ppermute | solution.py:16
  319.4 2.4 collective-permute-start.4
  322.9 1.9 constant_dynamic-update-slice_fusion.2
  324.8 1.9 constant_dynamic-update-slice_fusion.1
  326.7 14.5 %collective-permute-done.4 = bf16[256,1024]{1,0:T(8,128)(2,1)S(1)} collective-permute-done((bf16[256,1024]{1,0:T(8,128)(2,1)}, bf16[256,1024]{1,0:T(8,128)(2,1)S(1)}, u32[]{:S(2)}, u32[]{:S(2)}) %collective-permute-start.4) | collective-permute-done | bytes 524320 | tf_op jit(solution)/shard_map/ppermute | solution.py:16
  342.0 2.9 all-gather.16.cloned.1.call-done
  344.9 42.0 %all-gather.14.cloned.1.call-done = bf16[512,1024]{1,0:T(8,128)(2,1)} async-done(((bf16[128,1024]{1,0:T(8,128)(2,1)}), bf16[512,1024]{1,0:T(8,128)(2,1)}) %all-gather.14.cloned.1.call-update) | async-done | bytes 1048592 | tf_op jit(solution)/shard_map/all_gather | solution.py:229
  386.9 9.8 %convolution_convert_fusion.1 = bf16[512,1024]{1,0:T(8,128)(2,1)} fusion(bf16[1024,1024]{1,0:T(8,128)(2,1)} %all-gather.16.cloned.1.call-done, bf16[512,1024]{1,0:T(8,128)(2,1)} %all-gather.14.cloned.1.call-done, bf16[1024,1024]{1,0:T(8,128)(2,1)} %constant_dynamic-update-slice_fusion), kind=kOutput, calls=%fused_computation.39 | convolution fusion | flops 2182086656 | bytes 6291456 | tf_op jit(solution)/shard_map/dot_general | solution.py:235
  397.1 1.6 reshape.176
  398.7 38.0 %all_to_all.5 = bf16[32,2,16,4,128]{4,3,2,1,0:T(4,128)(2,1)S(1)} all-to-all(bf16[32,2,16,4,128]{4,3,2,1,0:T(4,128)(2,1)} %reshape.176), channel_id=1, replica_groups=mesh['seq'=32,'row'=4,'col'=4] {'seq'}, dimensions={0} | all-to-all | bytes 2097152 | tf_op jit(solution)/shard_map/all_to_all | solution.py:128
  436.7 6.3 %reduce-scatter.5.cloned.1.call-done = bf16[128,1024]{1,0:T(8,128)(2,1)} async-done(((bf16[512,1024]{1,0:T(8,128)(2,1)}), bf16[128,1024]{1,0:T(8,128)(2,1)}) %reduce-scatter.5.cloned.1.call-update) | async-done | bytes 262160 | tf_op jit(solution)/shard_map/reduce_scatter | solution.py:234
  443.0 1.1 fusion.84
  444.1 1.2 multiply_reduce_fusion
  445.3 1.8 fusion.87
  447.1 1.0 copy.95
  (189 shorter events, 35.0 us)
Async XLA Ops:
  7.2 85.7 %copy-start = (bf16[1024,4,192]{0,2,1:T(8,128)(2,1)S(1)}, bf16[1024,4,192]{0,2,1:T(8,128)(2,1)}, u32[]{:S(2)}) copy-start(bf16[1024,4,192]{0,2,1:T(8,128)(2,1)} %param.16) | copy-start | bytes 4718596
  7.2 42.8 %all-gather.12.cloned.1.call-start = ((), (), s32[]{:S(2)}) async-start(), calls=%async_computation.3 | async-start | bytes 1966080 | tf_op jit(solution)/shard_map/all_gather | solution.py:99
  7.9 204.3 %all-gather.18.cloned.1.call-start = ((), (), s32[]{:S(2)}) async-start(), calls=%async_computation.8 | async-start | bytes 4325376 | tf_op jit(solution)/shard_map/all_gather | solution.py:40
  90.1 1.0 copy-start.3
  92.8 204.2 %reduce-scatter.3.cloned.1.call-start = ((), (), s32[]{:S(2)}) async-start(), calls=%async_computation.4 | async-start | bytes 1310720 | tf_op jit(solution)/shard_map/reduce_scatter | solution.py:219
  96.0 6.5 %copy-start.2 = (s32[1,16384]{1,0:T(1,128)S(1)}, s32[1,16384]{1,0:T(1,128)}, u32[]{:S(2)}) copy-start(s32[1,16384]{1,0:T(1,128)} %param.25) | copy-start | bytes 196612
  96.0 6.6 %copy-start.11 = (s32[1,128]{1,0:T(1,128)S(1)}, s32[1,128]{1,0:T(1,128)}, u32[]{:S(2)}) copy-start(s32[1,128]{1,0:T(1,128)} %param.26) | copy-start | bytes 1540
  98.1 39.5 %collective-permute-start = (bf16[256,4,128]{0,2,1:T(8,128)(2,1)}, bf16[256,4,128]{0,2,1:T(8,128)(2,1)}, u32[]{:S(2)}, u32[]{:S(2)}) collective-permute-start(bf16[256,4,128]{0,2,1:T(8,128)(2,1)} %get-tuple-element.234), channel_id=1, source_target_pairs={{0,16},{16,32},{32,48},{48,64},{64,80},{80,96},{96,112},{112,128},... | collective-permute-start | bytes 786440 | tf_op jit(solution)/shard_map/ppermute | solution.py:31
  101.1 36.5 %collective-permute-start.1 = (bf16[256,4,128]{0,2,1:T(8,128)(2,1)S(1)}, bf16[256,4,128]{0,2,1:T(8,128)(2,1)}, u32[]{:S(2)}, u32[]{:S(2)}) collective-permute-start(bf16[256,4,128]{0,2,1:T(8,128)(2,1)S(1)} %get-tuple-element.235), channel_id=1, source_target_pairs={{16,0},{32,16},{48,32},{64,48},{80,64},{96,80},{112,96},{128,112},... | collective-permute-start | bytes 786440 | tf_op jit(solution)/shard_map/ppermute | solution.py:34
  143.8 2.9 copy-start.4
  255.5 41.5 %copy-start.5 = (bf16[1,512,1024]{2,1,0:T(8,128)(2,1)S(1)}, bf16[1,512,1024]{2,1,0:T(8,128)(2,1)}, u32[]{:S(2)}) copy-start(bf16[1,512,1024]{2,1,0:T(8,128)(2,1)} %param.15) | copy-start | bytes 3145732
  256.9 42.3 %copy-start.7 = (f32[1024]{0:T(1024)S(1)}, f32[1024]{0:T(1024)}, u32[]{:S(2)}) copy-start(f32[1024]{0:T(1024)} %param.20) | copy-start | bytes 12292
  256.9 42.3 %copy-start.8 = (f32[1024]{0:T(1024)S(1)}, f32[1024]{0:T(1024)}, u32[]{:S(2)}) copy-start(f32[1024]{0:T(1024)} %param.19) | copy-start | bytes 12292
  259.5 85.4 %all-gather.16.cloned.1.call-start = ((), (), s32[]{:S(2)}) async-start(), calls=%async_computation.6 | async-start | bytes 2621440 | tf_op jit(solution)/shard_map/all_gather | solution.py:233
  260.0 126.8 %all-gather.14.cloned.1.call-start = ((), (), s32[]{:S(2)}) async-start(), calls=%async_computation.5 | async-start | bytes 1310720 | tf_op jit(solution)/shard_map/all_gather | solution.py:229
  299.3 22.6 %copy-start.12 = (s32[1,32,1]{1,2,0:T(1,128)S(1)}, s32[1,32,1]{1,2,0:T(1,128)}, u32[]{:S(2)}) copy-start(s32[1,32,1]{1,2,0:T(1,128)} %param.27) | copy-start | bytes 388
  301.1 7.6 %copy-start.6 = (bf16[256,1024]{1,0:T(8,128)(2,1)S(1)}, bf16[256,1024]{1,0:T(8,128)(2,1)}, u32[]{:S(2)}) copy-start(bf16[256,1024]{1,0:T(8,128)(2,1)} %param.21) | copy-start | bytes 1572868
  301.1 141.9 %reduce-scatter.5.cloned.1.call-start = ((), (), s32[]{:S(2)}) async-start(), calls=%async_computation.7 | async-start | bytes 1310720 | tf_op jit(solution)/shard_map/reduce_scatter | solution.py:234
  301.2 18.3 %collective-permute-start.2 = (bf16[256,1024]{1,0:T(8,128)(2,1)}, bf16[256,1024]{1,0:T(8,128)(2,1)}, u32[]{:S(2)}, u32[]{:S(2)}) collective-permute-start(bf16[256,1024]{1,0:T(8,128)(2,1)} %param.21), channel_id=1, source_target_pairs={{0,4},{4,8},{8,12},{12,0},{1,5},{5,9},{9,13},{13,1},{2,6},{6,10},{... | collective-permute-start | bytes 1572872 | tf_op jit(solution)/shard_map/ppermute | solution.py:16
  304.4 20.4 %collective-permute-start.3 = (bf16[256,1024]{1,0:T(8,128)(2,1)}, bf16[256,1024]{1,0:T(8,128)(2,1)}, u32[]{:S(2)}, u32[]{:S(2)}) collective-permute-start(bf16[256,1024]{1,0:T(8,128)(2,1)} %param.21), channel_id=1, source_target_pairs={{0,12},{4,0},{8,4},{12,8},{1,13},{5,1},{9,5},{13,9},{2,14},{6,2},{... | collective-permute-start | bytes 1572872 | tf_op jit(solution)/shard_map/ppermute | solution.py:19
  319.4 21.7 %collective-permute-start.4 = (bf16[256,1024]{1,0:T(8,128)(2,1)}, bf16[256,1024]{1,0:T(8,128)(2,1)S(1)}, u32[]{:S(2)}, u32[]{:S(2)}) collective-permute-start(bf16[256,1024]{1,0:T(8,128)(2,1)} %collective-permute-done.2), channel_id=1, source_target_pairs={{0,4},{4,8},{8,12},{12,0},{1,5},{5,9},{9,13},{13,1},{2,6},{6,10},{... | collective-permute-start | bytes 1572872 | tf_op jit(solution)/shard_map/ppermute | solution.py:16
  397.1 45.9 %copy-start.1 = (bf16[128,1024]{1,0:T(8,128)(2,1)S(1)}, bf16[128,1024]{1,0:T(8,128)(2,1)}, u32[]{:S(2)}) copy-start(bf16[128,1024]{1,0:T(8,128)(2,1)} %add_convert_fusion.1) | copy-start | bytes 786436
  398.7 46.6 %copy-start.9 = (f32[1024]{0:T(1024)S(1)}, f32[1024]{0:T(1024)}, u32[]{:S(2)}) copy-start(f32[1024]{0:T(1024)} %param.24) | copy-start | bytes 12292
  398.7 46.6 %copy-start.10 = (f32[1024]{0:T(1024)S(1)}, f32[1024]{0:T(1024)}, u32[]{:S(2)}) copy-start(f32[1024]{0:T(1024)} %param.23) | copy-start | bytes 12292
Sparse Core Ops, SparseCore 0:
  10.1 39.8 all-gather.11
  92.9 67.9 all-gather.17
  259.6 37.3 reduce-scatter.2
  299.1 45.6 all-gather.15
  347.6 39.2 all-gather.13
  396.8 46.1 reduce-scatter.4
